TPU v7x, 32 devices: a whole 2x2x4 slice. The times are simulated.
32 devices in a mesh: users: 16 (over z, x, core), ctx: 2 (over y).
Axes of the slice: x: 2, y: 2, z: 4, core: 2. Of those that a mesh axis runs over, the one named last changes fastest.
Arguments:
- event_embed: bfloat16 [512, 16, 2048], P(('users', 'ctx')), may hold values from -6 to 6
- event_time_bucket: int32 [16, 2048], P('users', 'ctx'), may hold values from 0 to 127
- time_table: float32 [128, 512], replicated, may hold values from -6 to 6
- history_length: int32 [16], P('users'), may hold values from 512 to 2048, as said below
- w_proj: bfloat16 [512, 2048], replicated, may hold values from -0.25 to 0.25
- w_out: bfloat16 [512, 512], replicated, may hold values from -0.25 to 0.25
Outputs:
- layer_out: bfloat16 [16, 2048, 512], P('users', 'ctx')
Inputs may be any that keep to these rules, and one draw needn't show every extreme that they name: `history_length`: one user in every draw has a full history of 2048 events.
All inputs are finite; a program needn't handle non-finite values.
Results may differ from a plain program's by a relative error of at most 0.0068.
Values may be sent and summed in bfloat16 or wider, within the bound.
A program may use at most 64 MiB of HBM per device.

v0:
```python
import functools

import jax
import jax.numpy as jnp
from jax import lax
from jax.experimental import pallas as pl
from jax.experimental.pallas import tpu as pltpu
from jax.sharding import PartitionSpec as P

H = 8
BAND = 512
PREFIX = 512
TILE = 256
MESH = pl.DeviceIdType.MESH
F32 = jnp.float32
BF16 = jnp.bfloat16


def exchange_kernel(users, local_len, src, bucket, recv, bucket_out, own_sems, send_sems, recv_sems, relay_send, relay_recv, bucket_sems):
    u = lax.axis_index("users")
    c = lax.axis_index("ctx")
    other = 1 - c

    barrier = pltpu.get_barrier_semaphore()

    def greet(k, carry):
        pl.semaphore_signal(barrier, inc=1, device_id=(lax.rem(u + k, users), c), device_id_type=MESH)
        return carry

    lax.fori_loop(1, users, greet, 0)
    pl.semaphore_signal(barrier, inc=1, device_id=(u, other), device_id_type=MESH)
    pl.semaphore_wait(barrier, users)

    def scatter(k):
        return pltpu.make_async_remote_copy(
            src_ref=src.at[lax.rem(u + k, users)],
            dst_ref=recv.at[u, c],
            send_sem=send_sems.at[k],
            recv_sem=recv_sems.at[k],
            device_id=(lax.rem(u + k, users), c),
            device_id_type=MESH,
        )

    def start_scatter(k, carry):
        scatter(k).start()
        return carry

    lax.fori_loop(1, users, start_scatter, 0)

    def relay(slot_ref, dst, k):
        return pltpu.make_async_remote_copy(
            src_ref=slot_ref,
            dst_ref=dst,
            send_sem=relay_send.at[k],
            recv_sem=relay_recv.at[k],
            device_id=(u, other),
            device_id_type=MESH,
        )

    def full(s, k):
        return relay(recv.at[s, c], recv.at[s, c], k)

    def part(s, k):
        return relay(recv.at[s, c, :, pl.ds(0, local_len)], recv.at[s, c, :, pl.ds(0, local_len)], k)

    keep = pltpu.make_async_copy(src.at[u], recv.at[u, c], own_sems.at[0])
    keep.start()
    bucket_keep = pltpu.make_async_copy(bucket, bucket_out.at[c], own_sems.at[1])
    bucket_keep.start()
    bucket_send = pltpu.make_async_remote_copy(
        src_ref=bucket,
        dst_ref=bucket_out.at[c],
        send_sem=bucket_sems.at[0],
        recv_sem=bucket_sems.at[1],
        device_id=(u, other),
        device_id_type=MESH,
    )
    bucket_send.start()

    def own_full():
        return relay(src.at[u], recv.at[u, c], 0)

    def own_part():
        return relay(src.at[u, :, pl.ds(0, local_len)], recv.at[u, c, :, pl.ds(0, local_len)], 0)

    pl.when(c == 0)(lambda: own_full().start())
    pl.when(c != 0)(lambda: own_part().start())

    def forward(k, carry):
        s = lax.rem(u + users - k, users)
        scatter(k).wait_recv()
        pl.when(c == 0)(lambda: full(s, k).start())
        pl.when(c != 0)(lambda: part(s, k).start())
        return carry

    lax.fori_loop(1, users, forward, 0)

    def finish(k, carry):
        scatter(k).wait_send()

        @pl.when(c == 0)
        def _():
            full(0, k).wait_send()
            part(0, k).wait_recv()

        @pl.when(c != 0)
        def _():
            part(0, k).wait_send()
            full(0, k).wait_recv()

        return carry

    lax.fori_loop(1, users, finish, 0)

    @pl.when(c == 0)
    def _():
        own_full().wait_send()
        own_part().wait_recv()

    @pl.when(c != 0)
    def _():
        own_part().wait_send()
        own_full().wait_recv()

    bucket_send.wait()
    bucket_keep.wait()
    keep.wait()


def exchange(by_user, bucket):
    users, width, events = by_user.shape
    local_len = bucket.shape[-1]
    return pl.pallas_call(
        functools.partial(exchange_kernel, users, local_len),
        out_shape=(
            jax.ShapeDtypeStruct((users, 2, width, events), BF16),
            jax.ShapeDtypeStruct((2, 1, local_len), jnp.int32),
        ),
        in_specs=[pl.BlockSpec(memory_space=pl.ANY)] * 2,
        out_specs=(pl.BlockSpec(memory_space=pl.ANY),) * 2,
        scratch_shapes=[
            pltpu.SemaphoreType.DMA((2,)),
            pltpu.SemaphoreType.DMA((users,)),
            pltpu.SemaphoreType.DMA((users,)),
            pltpu.SemaphoreType.DMA((users,)),
            pltpu.SemaphoreType.DMA((users,)),
            pltpu.SemaphoreType.DMA((2,)),
        ],
        compiler_params=pltpu.CompilerParams(collective_id=0, has_side_effects=True),
        name="exchange",
    )(by_user, bucket)


def silu(v):
    half = v * 0.5
    return half + half * jnp.tanh(half)


def gain(u):
    return u + u * jnp.tanh(u)


def dot(a, b):
    return jnp.dot(a, b, preferred_element_type=F32)


def dot_t(a, b):
    return lax.dot_general(a, b, (((1,), (1,)), ((), ())), preferred_element_type=F32)


def layer_kernel(wide, cols, bucket, table, length, w_proj, w_out, out, tab, keys, vals, queries, gates, gated):
    c = lax.axis_index("ctx")
    width = cols.shape[0]
    blocks = cols.shape[1] // TILE
    local_len = out.shape[0]
    strips = local_len // TILE
    own = (PREFIX + BAND) // TILE if wide else c * strips
    buckets = table.shape[0]
    head = width // H
    pair = 2 * head

    flipped = table[...].T
    upper = flipped.astype(BF16)
    tab[:, :buckets] = upper
    tab[:, buckets:] = (flipped - upper.astype(F32)).astype(BF16)

    def rows_of(b):
        ids = bucket[b]
        hot = (lax.broadcasted_iota(jnp.int32, (buckets, TILE), 0) == ids).astype(F32).astype(BF16)
        span = pl.ds(pl.multiple_of(b * TILE, TILE), TILE)
        events = cols[:, span].astype(F32) + dot(tab[...], jnp.concatenate([hot, hot], axis=0))
        mean_square = jnp.sum(events * events, axis=0, keepdims=True) * (1.0 / width)
        return (events * lax.rsqrt(mean_square + 1e-05)).astype(BF16).T

    def project_block(b):
        span = pl.ds(pl.multiple_of(b * TILE, TILE), TILE)
        normed = rows_of(b)
        vals[span, :] = silu(dot(normed, w_proj[:, width : 2 * width])).astype(BF16)
        keys[span, :] = silu(dot(normed, w_proj[:, 3 * width :])).astype(BF16)
        mine = (b >= own) & (b < own + strips)

        @pl.when(mine)
        def _():
            row = pl.ds(pl.multiple_of((b - own) * TILE, TILE), TILE)
            gates[row, :] = silu(dot(normed, w_proj[:, :width])).astype(BF16)
            queries[row, :] = silu(dot(normed, w_proj[:, 2 * width : 3 * width])).astype(BF16) * 0.5

    first = jnp.where(c == 0, own, 0)
    last = jnp.where(c == 0, own + strips, blocks)

    def project_step(b, carry):
        project_block(b)
        return carry

    lax.fori_loop(first, last, project_step, 0)

    lane = lax.broadcasted_iota(jnp.int32, (1, pair), 1)
    row_id = lax.broadcasted_iota(jnp.int32, (TILE, TILE), 0)
    col_id = lax.broadcasted_iota(jnp.int32, (TILE, TILE), 1)
    lower = row_id >= col_id

    def halves(rows):
        zero = jnp.zeros_like(rows)
        return jnp.where(lane < head, rows, zero), jnp.where(lane < head, zero, rows)

    def strip(s, carry):
        row = pl.ds(pl.multiple_of(s * TILE, TILE), TILE)
        position = c * local_len + s * TILE + lax.broadcasted_iota(jnp.int32, (TILE, 1), 0)
        count = jnp.minimum(position + 1, PREFIX + BAND).astype(F32)
        factor = jnp.where(position < length[0], 1.0 / count, 0.0)

        def put(p, attended):
            at = slice(p * pair, (p + 1) * pair)
            gated[:, at] = (attended * factor * gates[row, at].astype(F32)).astype(BF16)

        def at_block(ref, b, p, n=1):
            return ref[pl.ds(pl.multiple_of(b * TILE, TILE), n * TILE), p * pair : (p + 1) * pair]

        @pl.when(c == 0)
        def _():
            for p in range(H // 2):
                qs = halves(queries[row, p * pair : (p + 1) * pair])
                vs = halves(at_block(vals, own + s, p))
                k = at_block(keys, own + s, p)
                acc = jnp.zeros((TILE, pair), F32)
                for h in range(2):
                    w = jnp.where(lower, gain(dot_t(qs[h], k)), 0.0).astype(BF16)
                    acc = acc + dot(w, vs[h])

                def step(j, acc):
                    vs = halves(at_block(vals, own + j, p))
                    k = at_block(keys, own + j, p)
                    for h in range(2):
                        acc = acc + dot(gain(dot_t(qs[h], k)).astype(BF16), vs[h])
                    return acc

                put(p, lax.fori_loop(0, s, step, acc))

        @pl.when(c != 0)
        def _():
            for p in range(H // 2):
                qs = halves(queries[row, p * pair : (p + 1) * pair])
                k_pre = at_block(keys, 0, p, PREFIX // TILE)
                v_pre = halves(at_block(vals, 0, p, PREFIX // TILE))
                span = BAND // TILE
                k_win = at_block(keys, own + s - span, p, span + 1)
                v_win = halves(at_block(vals, own + s - span, p, span + 1))
                acc = jnp.zeros((TILE, pair), F32)
                for h in range(2):
                    acc = acc + dot(gain(dot_t(qs[h], k_pre)).astype(BF16), v_pre[h])
                    scores = dot_t(qs[h], k_win)
                    middle = gain(scores[:, TILE : span * TILE]).astype(BF16)
                    ends = gain(jnp.where(lower, scores[:, span * TILE :], scores[:, :TILE]))
                    oldest = jnp.where(lower, 0.0, ends).astype(BF16)
                    newest = jnp.where(lower, ends, 0.0).astype(BF16)
                    acc = acc + dot(jnp.concatenate([oldest, middle, newest], axis=1), v_win[h])
                put(p, acc)

        out[row, :] = dot(gated[...], w_out[...]).astype(BF16)
        return carry

    lax.fori_loop(0, strips, strip, 0)


def layer(wide, cols, bucket, table, length, w_proj, w_out, local_len):
    width, events = cols.shape
    vmem = pl.BlockSpec(memory_space=pltpu.VMEM)
    return pl.pallas_call(
        functools.partial(layer_kernel, wide),
        out_shape=jax.ShapeDtypeStruct((local_len, width), BF16),
        in_specs=[vmem, vmem, vmem, pl.BlockSpec(memory_space=pltpu.SMEM), vmem, vmem],
        out_specs=vmem,
        scratch_shapes=[
            pltpu.VMEM((width, 2 * table.shape[0]), BF16),
            pltpu.VMEM((events, width), BF16),
            pltpu.VMEM((events, width), BF16),
            pltpu.VMEM((local_len, width), BF16),
            pltpu.VMEM((local_len, width), BF16),
            pltpu.VMEM((TILE, width), BF16),
        ],
        name="layer",
    )(cols, bucket.reshape(-1, 1, TILE), table, length, w_proj, w_out)


def gather_wide(event_embed, bucket, ctx):
    local_len = bucket.shape[1]
    rows = lax.all_to_all(event_embed, "users", split_axis=1, concat_axis=0, tiled=True)[:, 0]
    users = lax.axis_size("users")
    all_buckets = lax.all_gather(bucket, "ctx", axis=1, tiled=True)
    start = lax.axis_index("ctx") * local_len

    def pieces(array, at):
        older = jnp.pad(array, ((0, 0), (BAND, 0)))
        band = lax.dynamic_slice_in_dim(older, at, BAND, 1)
        return jnp.concatenate([array[:, :PREFIX], band, lax.dynamic_slice_in_dim(array, at, local_len, 1)], axis=1)

    parts = jnp.stack([pieces(rows, at * local_len) for at in range(ctx)])
    got = lax.all_to_all(parts, "ctx", split_axis=0, concat_axis=0, tiled=True)
    width, span = got.shape[1] // users, got.shape[2]
    cols = got.reshape(ctx, users, width, span).transpose(1, 0, 2, 3).reshape(-1, span)
    return cols, pieces(all_buckets, start)


def local(event_embed, event_time_bucket, time_table, history_length, w_proj, w_out):
    ctx = lax.axis_size("ctx")
    local_len = event_time_bucket.shape[1]
    wide = ctx != 2 or ctx * local_len != PREFIX + BAND + local_len
    if wide:
        cols, bucket = gather_wide(event_embed, event_time_bucket, ctx)
    else:
        slots, bucket = exchange(event_embed.transpose(1, 0, 2), event_time_bucket)
        cols = slots.reshape(-1, slots.shape[-1])
    return layer(wide, cols, bucket, time_table, history_length, w_proj, w_out, local_len)[None]


def solution(mesh):
    return jax.shard_map(
        local,
        mesh=mesh,
        in_specs=(P(("users", "ctx"), None, None), P("users", "ctx"), P(), P("users"), P(), P()),
        out_specs=P("users", "ctx", None),
        check_vma=False,
    )
```

profile of v0, /device:TPU:24, one launch (start us, length us, event | category | flops | bytes accessed | tf_op | source)
XLA Modules:
  0.0 72.1 jit_solution(2876164493438021669)
XLA Ops:
  0.0 2.8 %copy.9 = bf16[16,16,2048]{2,0,1:T(8,128)(2,1)} copy(bf16[16,16,2048]{2,1,0:T(8,128)(2,1)} %param.6) | data formatting | bytes 2097152 | tf_op args[0]
  2.8 39.5 %exchange.1 = (bf16[16,2,16,2048]{3,2,1,0:T(8,128)(2,1)}, s32[2,1,1024]{2,1,0:T(1,128)}) custom-call(bf16[16,16,2048]{2,1,0:T(8,128)(2,1)} %bitcast.6, s32[1,1024]{1,0:T(1,128)} %bucket.1), custom_call_target="tpu_custom_call" | custom-call | tf_op jit(solution)/shard_map/exchange/pallas_call | solution.py:133
  42.9 29.2 %layer.1 = bf16[1024,512]{1,0:T(8,128)(2,1)} custom-call(bf16[512,2048]{1,0:T(8,128)(2,1)} %bitcast.7, s32[8,1,256]{2,1,0:T(1,128)} %bitcast.8, f32[128,512]{1,0:T(8,128)} %table.1, s32[1]{0:T(128)S(6)} %copy.10.length, bf16[512,2048]{1,0:T(8,128)(2,1)} %w_proj.1, bf16[512,512]{1,0:T(8,128)(2,1)} %w_out.1), custom_call_target="tpu_custom_call" | custom-call | tf_op jit(solution)/shard_map/layer/pallas_call | solution.py:288
where the time goes:
time: 72.3 us; the launch traced here: 72.1 us
  Pallas kernels  68.7 us (95%)
  local copies, waits for them, and re-layouts  2.77 us (4%)
    pallas_call x1, Pallas kernels, exchange(): pl.pallas_call(functools.partial(exchange_kernel, users, local_len), out_...  39.5 us
    pallas_call x1, Pallas kernels, layer(): pl.pallas_call(functools.partial(layer_kernel, wide), out_shape=jax.Shape...  29.2 us
    unnamed x1, local copies, waits for them, and re-layouts  2.77 us

commit v1 on v0

--- a/solution.py
+++ b/solution.py
@@ -24,7 +24,7 @@
     barrier = pltpu.get_barrier_semaphore()
 
     def greet(k, carry):
-        pl.semaphore_signal(barrier, inc=1, device_id=(lax.rem(u + k, users), c), device_id_type=MESH)
+        pl.semaphore_signal(barrier, inc=1, device_id=(u ^ k, c), device_id_type=MESH)
         return carry
 
     lax.fori_loop(1, users, greet, 0)
@@ -33,11 +33,11 @@
 
     def scatter(k):
         return pltpu.make_async_remote_copy(
-            src_ref=src.at[lax.rem(u + k, users)],
+            src_ref=src.at[u ^ k],
             dst_ref=recv.at[u, c],
             send_sem=send_sems.at[k],
             recv_sem=recv_sems.at[k],
-            device_id=(lax.rem(u + k, users), c),
+            device_id=(u ^ k, c),
             device_id_type=MESH,
         )
 
@@ -87,7 +87,7 @@
     pl.when(c != 0)(lambda: own_part().start())
 
     def forward(k, carry):
-        s = lax.rem(u + users - k, users)
+        s = u ^ k
         scatter(k).wait_recv()
         pl.when(c == 0)(lambda: full(s, k).start())
         pl.when(c != 0)(lambda: part(s, k).start())
@@ -324,7 +324,8 @@
 def local(event_embed, event_time_bucket, time_table, history_length, w_proj, w_out):
     ctx = lax.axis_size("ctx")
     local_len = event_time_bucket.shape[1]
-    wide = ctx != 2 or ctx * local_len != PREFIX + BAND + local_len
+    users = lax.axis_size("users")
+    wide = ctx != 2 or ctx * local_len != PREFIX + BAND + local_len or users & (users - 1) != 0
     if wide:
         cols, bucket = gather_wide(event_embed, event_time_bucket, ctx)
     else:

time: 72.3 us -> 66.3 us (0.917)
  the two profiles are of different devices: /device:TPU:24 before, /device:TPU:0 now
where the time goes in v1:
time: 66.3 us; the launch traced here: 66.2 us
  Pallas kernels  62.8 us (95%)
  local copies, waits for them, and re-layouts  2.77 us (4%)
    pallas_call x1, Pallas kernels, exchange(): pl.pallas_call(functools.partial(exchange_kernel, users, local_len), out_...  33.6 us
    pallas_call x1, Pallas kernels, layer(): pl.pallas_call(functools.partial(layer_kernel, wide), out_shape=jax.Shape...  29.2 us
    unnamed x1, local copies, waits for them, and re-layouts  2.77 us

profile of v1, /device:TPU:0, one launch (start us, length us, event | category | flops | bytes accessed | tf_op | source)
XLA Modules:
  0.0 66.2 jit_solution(15116614147572664754)
XLA Ops:
  0.0 2.8 %copy.9 = bf16[16,16,2048]{2,0,1:T(8,128)(2,1)} copy(bf16[16,16,2048]{2,1,0:T(8,128)(2,1)} %param.6) | data formatting | bytes 2097152 | tf_op args[0]
  2.8 33.6 %exchange.1 = (bf16[16,2,16,2048]{3,2,1,0:T(8,128)(2,1)}, s32[2,1,1024]{2,1,0:T(1,128)}) custom-call(bf16[16,16,2048]{2,1,0:T(8,128)(2,1)} %bitcast.6, s32[1,1024]{1,0:T(1,128)} %bucket.1), custom_call_target="tpu_custom_call" | custom-call | tf_op jit(solution)/shard_map/exchange/pallas_call | solution.py:133
  37.0 29.2 %layer.1 = bf16[1024,512]{1,0:T(8,128)(2,1)} custom-call(bf16[512,2048]{1,0:T(8,128)(2,1)} %bitcast.7, s32[8,1,256]{2,1,0:T(1,128)} %bitcast.8, f32[128,512]{1,0:T(8,128)} %table.1, s32[1]{0:T(128)S(6)} %copy.10.length, bf16[512,2048]{1,0:T(8,128)(2,1)} %w_proj.1, bf16[512,512]{1,0:T(8,128)(2,1)} %w_out.1), custom_call_target="tpu_custom_call" | custom-call | tf_op jit(solution)/shard_map/layer/pallas_call | solution.py:288

commit v2 on v1

v2 whole, which is shorter than its diff:
```python
import functools

import jax
import jax.numpy as jnp
from jax import lax
from jax.experimental import pallas as pl
from jax.experimental.pallas import tpu as pltpu
from jax.sharding import PartitionSpec as P

H = 8
BAND = 512
PREFIX = 512
TILE = 256
MESH = pl.DeviceIdType.MESH
F32 = jnp.float32
BF16 = jnp.bfloat16


def silu(v):
    half = v * 0.5
    return half + half * jnp.tanh(half)


def gain(u):
    return u + u * jnp.tanh(u)


def dot(a, b):
    return jnp.dot(a, b, preferred_element_type=F32)


def dot_t(a, b):
    return lax.dot_general(a, b, (((1,), (1,)), ((), ())), preferred_element_type=F32)


def steps_of(c, own, strips, cols_at, bucket_at, table, length, w_proj, w_out, out, tab, keys, vals, queries, gates, gated):
    width = w_out.shape[0]
    local_len = out.shape[0]
    buckets = table.shape[0]
    head = width // H
    pair = 2 * head

    flipped = table[...].T
    upper = flipped.astype(BF16)
    tab[:, :buckets] = upper
    tab[:, buckets:] = (flipped - upper.astype(F32)).astype(BF16)

    def rows_of(b):
        ids = bucket_at(b)
        hot = (lax.broadcasted_iota(jnp.int32, (buckets, TILE), 0) == ids).astype(F32).astype(BF16)
        span = pl.ds(pl.multiple_of(b * TILE, TILE), TILE)
        events = cols_at(span).astype(F32) + dot(tab[...], jnp.concatenate([hot, hot], axis=0))
        mean_square = jnp.sum(events * events, axis=0, keepdims=True) * (1.0 / width)
        return (events * lax.rsqrt(mean_square + 1e-05)).astype(BF16).T

    def project_block(b):
        span = pl.ds(pl.multiple_of(b * TILE, TILE), TILE)
        normed = rows_of(b)
        vals[span, :] = silu(dot(normed, w_proj[:, width : 2 * width])).astype(BF16)
        keys[span, :] = silu(dot(normed, w_proj[:, 3 * width :])).astype(BF16)
        mine = (b >= own) & (b < own + strips)

        @pl.when(mine)
        def _():
            row = pl.ds(pl.multiple_of((b - own) * TILE, TILE), TILE)
            gates[row, :] = silu(dot(normed, w_proj[:, :width])).astype(BF16)
            queries[row, :] = silu(dot(normed, w_proj[:, 2 * width : 3 * width])).astype(BF16) * 0.5

    lane = lax.broadcasted_iota(jnp.int32, (1, pair), 1)
    row_id = lax.broadcasted_iota(jnp.int32, (TILE, TILE), 0)
    col_id = lax.broadcasted_iota(jnp.int32, (TILE, TILE), 1)
    lower = row_id >= col_id

    def halves(rows):
        zero = jnp.zeros_like(rows)
        return jnp.where(lane < head, rows, zero), jnp.where(lane < head, zero, rows)

    def strip(s, early):
        row = pl.ds(pl.multiple_of(s * TILE, TILE), TILE)
        position = c * local_len + s * TILE + lax.broadcasted_iota(jnp.int32, (TILE, 1), 0)
        count = jnp.minimum(position + 1, PREFIX + BAND).astype(F32)
        factor = jnp.where(position < length[0], 1.0 / count, 0.0)

        def put(p, attended):
            at = slice(p * pair, (p + 1) * pair)
            gated[:, at] = (attended * factor * gates[row, at].astype(F32)).astype(BF16)

        def at_block(ref, b, p, n=1):
            return ref[pl.ds(pl.multiple_of(b * TILE, TILE), n * TILE), p * pair : (p + 1) * pair]

        def early_pairs():
            for p in range(H // 2):
                qs = halves(queries[row, p * pair : (p + 1) * pair])
                vs = halves(at_block(vals, own + s, p))
                k = at_block(keys, own + s, p)
                acc = jnp.zeros((TILE, pair), F32)
                for h in range(2):
                    w = jnp.where(lower, gain(dot_t(qs[h], k)), 0.0).astype(BF16)
                    acc = acc + dot(w, vs[h])

                def step(j, acc):
                    vs = halves(at_block(vals, own + j, p))
                    k = at_block(keys, own + j, p)
                    for h in range(2):
                        acc = acc + dot(gain(dot_t(qs[h], k)).astype(BF16), vs[h])
                    return acc

                put(p, lax.fori_loop(0, s, step, acc))

        def later_pairs():
            for p in range(H // 2):
                qs = halves(queries[row, p * pair : (p + 1) * pair])
                k_pre = at_block(keys, 0, p, PREFIX // TILE)
                v_pre = halves(at_block(vals, 0, p, PREFIX // TILE))
                span = BAND // TILE
                k_win = at_block(keys, own + s - span, p, span + 1)
                v_win = halves(at_block(vals, own + s - span, p, span + 1))
                acc = jnp.zeros((TILE, pair), F32)
                for h in range(2):
                    acc = acc + dot(gain(dot_t(qs[h], k_pre)).astype(BF16), v_pre[h])
                    scores = dot_t(qs[h], k_win)
                    middle = gain(scores[:, TILE : span * TILE]).astype(BF16)
                    ends = gain(jnp.where(lower, scores[:, span * TILE :], scores[:, :TILE]))
                    oldest = jnp.where(lower, 0.0, ends).astype(BF16)
                    newest = jnp.where(lower, ends, 0.0).astype(BF16)
                    acc = acc + dot(jnp.concatenate([oldest, middle, newest], axis=1), v_win[h])
                put(p, acc)

        (early_pairs if early else later_pairs)()
        out[row, :] = dot(gated[...], w_out[...]).astype(BF16)

    return project_block, strip


def each(first, last, body):
    def step(i, carry):
        body(i)
        return carry

    lax.fori_loop(first, last, step, 0)


def layer_kernel(cols, bucket, table, length, w_proj, w_out, out, *scratch):
    c = lax.axis_index("ctx")
    blocks = cols.shape[1] // TILE
    strips = out.shape[0] // TILE
    own = (PREFIX + BAND) // TILE
    project_block, strip = steps_of(
        c, own, strips, lambda span: cols[:, span], lambda b: bucket[b], table, length, w_proj, w_out, out, *scratch
    )
    each(jnp.where(c == 0, own, 0), jnp.where(c == 0, own + strips, blocks), project_block)

    @pl.when(c == 0)
    def _():
        each(0, strips, lambda s: strip(s, True))

    @pl.when(c != 0)
    def _():
        each(0, strips, lambda s: strip(s, False))


def fused_kernel(
    users, src, bucket, table, length, w_proj, w_out, out,
    recv, ids, own_sems, send_sems, recv_sems, relay_send, relay_recv, bucket_sems, *scratch,
):
    u = lax.axis_index("users")
    c = lax.axis_index("ctx")
    other = 1 - c
    local_len = out.shape[0]
    half = local_len // 2
    strips = local_len // TILE

    def span_of(ch):
        if isinstance(ch, int) and ch == 0:
            return pl.ds(0, local_len)
        return pl.ds(pl.multiple_of(local_len + (ch - 1) * half, half), half)

    barrier = pltpu.get_barrier_semaphore()
    each(1, users, lambda k: pl.semaphore_signal(barrier, inc=1, device_id=(u ^ k, c), device_id_type=MESH))
    pl.semaphore_signal(barrier, inc=1, device_id=(u, other), device_id_type=MESH)
    pl.semaphore_wait(barrier, users)

    def scatter(ch, k):
        return pltpu.make_async_remote_copy(
            src_ref=src.at[u ^ k, :, span_of(ch)],
            dst_ref=recv.at[u, c, :, span_of(ch)],
            send_sem=send_sems.at[ch, k],
            recv_sem=recv_sems.at[ch, k],
            device_id=(u ^ k, c),
            device_id_type=MESH,
        )

    def relay(ch, k):
        return pltpu.make_async_remote_copy(
            src_ref=recv.at[u ^ k, c, :, span_of(ch)],
            dst_ref=recv.at[u ^ k, c, :, span_of(ch)],
            send_sem=relay_send.at[ch, k],
            recv_sem=relay_recv.at[ch, k],
            device_id=(u, other),
            device_id_type=MESH,
        )

    def incoming(ch, k):
        return pltpu.make_async_remote_copy(
            src_ref=recv.at[u ^ k, other, :, span_of(ch)],
            dst_ref=recv.at[u ^ k, other, :, span_of(ch)],
            send_sem=relay_send.at[ch, k],
            recv_sem=relay_recv.at[ch, k],
            device_id=(u, other),
            device_id_type=MESH,
        )

    keep = pltpu.make_async_copy(src.at[u], recv.at[u, c], own_sems.at[0])
    keep.start()
    id_keep = pltpu.make_async_copy(bucket, ids.at[c], own_sems.at[1])
    id_keep.start()
    id_send = pltpu.make_async_remote_copy(
        src_ref=bucket,
        dst_ref=ids.at[c],
        send_sem=bucket_sems.at[0],
        recv_sem=bucket_sems.at[1],
        device_id=(u, other),
        device_id_type=MESH,
    )
    id_send.start()
    for ch in range(3):
        each(1, users, lambda k: scatter(ch, k).start())
    keep.wait()
    relay(0, 0).start()

    def forward(ch):
        def one(k):
            scatter(ch, k).wait_recv()
            relay(ch, k).start()

        each(1, users, one)

    forward(0)
    id_keep.wait()
    id_send.wait()
    each(0, users, lambda k: incoming(0, k).wait_recv())

    def cols_at(span):
        return recv[:, :, :, span].reshape(w_out.shape[0], TILE)

    def ids_at(b):
        return ids[b // strips, :, pl.ds(pl.multiple_of(lax.rem(b, strips) * TILE, TILE), TILE)]

    project_block, strip = steps_of(
        c, c * strips, strips, cols_at, ids_at, table, length, w_proj, w_out, out, *scratch
    )
    part = strips // 2

    @pl.when(c == 0)
    def _():
        def phase(ph):
            each(ph * part, (ph + 1) * part, project_block)
            relay(ph + 1, 0).start()
            forward(ph + 1)
            each(ph * part, (ph + 1) * part, lambda s: strip(s, True))

        each(0, 2, phase)

        def sent(k):
            relay(1, k).wait_send()
            relay(2, k).wait_send()

        each(0, users, sent)

    @pl.when(c != 0)
    def _():
        each(0, strips, project_block)

        def phase(ph):
            each(1, users, lambda k: scatter(ph + 1, k).wait_recv())
            each(0, users, lambda k: incoming(ph + 1, k).wait_recv())
            each(strips + ph * part, strips + (ph + 1) * part, project_block)
            each(ph * part, (ph + 1) * part, lambda s: strip(s, False))

        each(0, 2, phase)

    each(0, users, lambda k: relay(0, k).wait_send())
    for ch in range(3):
        each(1, users, lambda k: scatter(ch, k).wait_send())


def fused(by_user, bucket, table, length, w_proj, w_out):
    users, cols, events = by_user.shape
    width = w_out.shape[0]
    local_len = bucket.shape[-1]
    vmem = pl.BlockSpec(memory_space=pltpu.VMEM)
    far = pl.BlockSpec(memory_space=pl.ANY)
    sems = pltpu.SemaphoreType.DMA((3, users))
    return pl.pallas_call(
        functools.partial(fused_kernel, users),
        out_shape=jax.ShapeDtypeStruct((local_len, width), BF16),
        in_specs=[far, far, vmem, pl.BlockSpec(memory_space=pltpu.SMEM), vmem, vmem],
        out_specs=vmem,
        scratch_shapes=[
            pltpu.VMEM((users, 2, cols, events), BF16),
            pltpu.VMEM((2, 1, local_len), jnp.int32),
            pltpu.SemaphoreType.DMA((2,)),
            sems,
            sems,
            sems,
            sems,
            pltpu.SemaphoreType.DMA((2,)),
            *layer_scratch(table, width, events, local_len),
        ],
        compiler_params=pltpu.CompilerParams(collective_id=0, has_side_effects=True),
        name="fused",
    )(by_user, bucket, table, length, w_proj, w_out)


def layer_scratch(table, width, events, local_len):
    return [
        pltpu.VMEM((width, 2 * table.shape[0]), BF16),
        pltpu.VMEM((events, width), BF16),
        pltpu.VMEM((events, width), BF16),
        pltpu.VMEM((local_len, width), BF16),
        pltpu.VMEM((local_len, width), BF16),
        pltpu.VMEM((TILE, width), BF16),
    ]


def layer(cols, bucket, table, length, w_proj, w_out, local_len):
    width, events = cols.shape
    vmem = pl.BlockSpec(memory_space=pltpu.VMEM)
    return pl.pallas_call(
        layer_kernel,
        out_shape=jax.ShapeDtypeStruct((local_len, width), BF16),
        in_specs=[vmem, vmem, vmem, pl.BlockSpec(memory_space=pltpu.SMEM), vmem, vmem],
        out_specs=vmem,
        scratch_shapes=layer_scratch(table, width, events, local_len),
        name="layer",
    )(cols, bucket.reshape(-1, 1, TILE), table, length, w_proj, w_out)


def gather_wide(event_embed, bucket, ctx):
    local_len = bucket.shape[1]
    rows = lax.all_to_all(event_embed, "users", split_axis=1, concat_axis=0, tiled=True)[:, 0]
    users = lax.axis_size("users")
    all_buckets = lax.all_gather(bucket, "ctx", axis=1, tiled=True)
    start = lax.axis_index("ctx") * local_len

    def pieces(array, at):
        older = jnp.pad(array, ((0, 0), (BAND, 0)))
        band = lax.dynamic_slice_in_dim(older, at, BAND, 1)
        return jnp.concatenate([array[:, :PREFIX], band, lax.dynamic_slice_in_dim(array, at, local_len, 1)], axis=1)

    parts = jnp.stack([pieces(rows, at * local_len) for at in range(ctx)])
    got = lax.all_to_all(parts, "ctx", split_axis=0, concat_axis=0, tiled=True)
    width, span = got.shape[1] // users, got.shape[2]
    cols = got.reshape(ctx, users, width, span).transpose(1, 0, 2, 3).reshape(-1, span)
    return cols, pieces(all_buckets, start)


def local(event_embed, event_time_bucket, time_table, history_length, w_proj, w_out):
    ctx = lax.axis_size("ctx")
    local_len = event_time_bucket.shape[1]
    users = lax.axis_size("users")
    wide = ctx != 2 or ctx * local_len != PREFIX + BAND + local_len or users & (users - 1) != 0
    if wide:
        cols, bucket = gather_wide(event_embed, event_time_bucket, ctx)
        done = layer(cols, bucket, time_table, history_length, w_proj, w_out, local_len)
    else:
        by_user = event_embed.transpose(1, 0, 2)
        done = fused(by_user, event_time_bucket, time_table, history_length, w_proj, w_out)
    return done[None]


def solution(mesh):
    return jax.shard_map(
        local,
        mesh=mesh,
        in_specs=(P(("users", "ctx"), None, None), P("users", "ctx"), P(), P("users"), P(), P()),
        out_specs=P("users", "ctx", None),
        check_vma=False,
    )
```

time: 66.3 us -> 65.7 us (level)
  the two profiles are of different devices: /device:TPU:0 before, /device:TPU:15 now
where the time goes in v2:
time: 65.7 us; the launch traced here: 65.3 us
  Pallas kernels  59.6 us (91%)
  local copies, waits for them, and re-layouts  5.04 us (8%)
  between operations  0.66 us (1%)
    pallas_call x1, Pallas kernels, fused(): pl.pallas_call(functools.partial(fused_kernel, users), out_shape=jax.Shap...  59.6 us
    unnamed x2, local copies, waits for them, and re-layouts  5.04 us

profile of v2, /device:TPU:15, one launch (start us, length us, event | category | flops | bytes accessed | tf_op | source)
XLA Modules:
  0.0 65.3 jit_solution(7251148651175522261)
XLA Ops:
  0.7 2.8 %copy.9 = bf16[16,16,2048]{2,0,1:T(8,128)(2,1)} copy(bf16[16,16,2048]{2,1,0:T(8,128)(2,1)} %param.6) | data formatting | bytes 2097152 | tf_op args[0]
  3.4 59.6 %fused.1 = bf16[1024,512]{1,0:T(8,128)(2,1)} custom-call(bf16[16,16,2048]{2,1,0:T(8,128)(2,1)} %bitcast.5, s32[1,1024]{1,0:T(1,128)} %bucket.1, f32[128,512]{1,0:T(8,128)} %table.1, s32[1]{0:T(128)S(6)} %copy.11.length, bf16[512,2048]{1,0:T(8,128)(2,1)} %w_proj.1, bf16[512,512]{1,0:T(8,128)(2,1)} %w_out.1), custom_call_target="tpu_custom_call" | custom-call | tf_op jit(solution)/shard_map/fused/pallas_call | solution.py:294
  63.1 2.3 %copy.12 = bf16[1,1024,512]{2,1,0:T(8,128)(2,1)} copy(bf16[1,1024,512]{2,1,0:T(8,128)(2,1)} %bitcast.4) | data formatting | bytes 2097152

commit v3 on v2

--- a/solution.py
+++ b/solution.py
@@ -93,19 +93,16 @@
                 qs = halves(queries[row, p * pair : (p + 1) * pair])
                 vs = halves(at_block(vals, own + s, p))
                 k = at_block(keys, own + s, p)
+                if s > 0:
+                    k_old = at_block(keys, own, p, s)
+                    v_old = halves(at_block(vals, own, p, s))
                 acc = jnp.zeros((TILE, pair), F32)
                 for h in range(2):
                     w = jnp.where(lower, gain(dot_t(qs[h], k)), 0.0).astype(BF16)
                     acc = acc + dot(w, vs[h])
-
-                def step(j, acc):
-                    vs = halves(at_block(vals, own + j, p))
-                    k = at_block(keys, own + j, p)
-                    for h in range(2):
-                        acc = acc + dot(gain(dot_t(qs[h], k)).astype(BF16), vs[h])
-                    return acc
-
-                put(p, lax.fori_loop(0, s, step, acc))
+                    if s > 0:
+                        acc = acc + dot(gain(dot_t(qs[h], k_old)).astype(BF16), v_old[h])
+                put(p, acc)
 
         def later_pairs():
             for p in range(H // 2):
@@ -152,7 +149,8 @@
 
     @pl.when(c == 0)
     def _():
-        each(0, strips, lambda s: strip(s, True))
+        for s in range(strips):
+            strip(s, True)
 
     @pl.when(c != 0)
     def _():
@@ -167,13 +165,12 @@
     c = lax.axis_index("ctx")
     other = 1 - c
     local_len = out.shape[0]
-    half = local_len // 2
     strips = local_len // TILE
 
     def span_of(ch):
         if isinstance(ch, int) and ch == 0:
             return pl.ds(0, local_len)
-        return pl.ds(pl.multiple_of(local_len + (ch - 1) * half, half), half)
+        return pl.ds(pl.multiple_of(local_len + (ch - 1) * TILE, TILE), TILE)
 
     barrier = pltpu.get_barrier_semaphore()
     each(1, users, lambda k: pl.semaphore_signal(barrier, inc=1, device_id=(u ^ k, c), device_id_type=MESH))
@@ -223,8 +220,8 @@
         device_id_type=MESH,
     )
     id_send.start()
-    for ch in range(3):
-        each(1, users, lambda k: scatter(ch, k).start())
+    each(1, users, lambda k: scatter(0, k).start())
+    each(1, strips + 1, lambda ch: each(1, users, lambda k: scatter(ch, k).start()))
     keep.wait()
     relay(0, 0).start()
 
@@ -253,19 +250,18 @@
 
     @pl.when(c == 0)
     def _():
-        def phase(ph):
-            each(ph * part, (ph + 1) * part, project_block)
-            relay(ph + 1, 0).start()
-            forward(ph + 1)
-            each(ph * part, (ph + 1) * part, lambda s: strip(s, True))
-
-        each(0, 2, phase)
-
-        def sent(k):
-            relay(1, k).wait_send()
-            relay(2, k).wait_send()
-
-        each(0, users, sent)
+        def pass_on(ch):
+            relay(ch, 0).start()
+            forward(ch)
+
+        each(0, part, project_block)
+        pass_on(1)
+        each(part, strips, project_block)
+        for s in range(strips):
+            if s + 2 <= strips:
+                pass_on(s + 2)
+            strip(s, True)
+        each(1, strips + 1, lambda ch: each(0, users, lambda k: relay(ch, k).wait_send()))
 
     @pl.when(c != 0)
     def _():
@@ -274,14 +270,14 @@
         def phase(ph):
             each(1, users, lambda k: scatter(ph + 1, k).wait_recv())
             each(0, users, lambda k: incoming(ph + 1, k).wait_recv())
-            each(strips + ph * part, strips + (ph + 1) * part, project_block)
-            each(ph * part, (ph + 1) * part, lambda s: strip(s, False))
-
-        each(0, 2, phase)
+            project_block(strips + ph)
+            strip(ph, False)
+
+        each(0, strips, phase)
 
     each(0, users, lambda k: relay(0, k).wait_send())
-    for ch in range(3):
-        each(1, users, lambda k: scatter(ch, k).wait_send())
+    each(1, users, lambda k: scatter(0, k).wait_send())
+    each(1, strips + 1, lambda ch: each(1, users, lambda k: scatter(ch, k).wait_send()))
 
 
 def fused(by_user, bucket, table, length, w_proj, w_out):
@@ -290,7 +286,7 @@
     local_len = bucket.shape[-1]
     vmem = pl.BlockSpec(memory_space=pltpu.VMEM)
     far = pl.BlockSpec(memory_space=pl.ANY)
-    sems = pltpu.SemaphoreType.DMA((3, users))
+    sems = pltpu.SemaphoreType.DMA((1 + local_len // TILE, users))
     return pl.pallas_call(
         functools.partial(fused_kernel, users),
         out_shape=jax.ShapeDtypeStruct((local_len, width), BF16),

time: 65.7 us -> 65.9 us (level)
  no operation moved by 1% of the time
where the time goes in v3:
time: 65.9 us; the launch traced here: 65.7 us
  Pallas kernels  60 us (91%)
  local copies, waits for them, and re-layouts  5.04 us (8%)
  between operations  0.66 us (1%)
    pallas_call x1, Pallas kernels, fused(): pl.pallas_call(functools.partial(fused_kernel, users), out_shape=jax.Shap...  60 us
    unnamed x2, local copies, waits for them, and re-layouts  5.04 us

profile of v3, /device:TPU:15, one launch (start us, length us, event | category | flops | bytes accessed | tf_op | source)
XLA Modules:
  0.0 65.7 jit_solution(17496411507435052991)
XLA Ops:
  0.7 2.8 %copy.9 = bf16[16,16,2048]{2,0,1:T(8,128)(2,1)} copy(bf16[16,16,2048]{2,1,0:T(8,128)(2,1)} %param.6) | data formatting | bytes 2097152 | tf_op args[0]
  3.4 60.0 %fused.1 = bf16[1024,512]{1,0:T(8,128)(2,1)} custom-call(bf16[16,16,2048]{2,1,0:T(8,128)(2,1)} %bitcast.5, s32[1,1024]{1,0:T(1,128)} %bucket.1, f32[128,512]{1,0:T(8,128)} %table.1, s32[1]{0:T(128)S(6)} %copy.11.length, bf16[512,2048]{1,0:T(8,128)(2,1)} %w_proj.1, bf16[512,512]{1,0:T(8,128)(2,1)} %w_out.1), custom_call_target="tpu_custom_call" | custom-call | tf_op jit(solution)/shard_map/fused/pallas_call | solution.py:290
  63.4 2.3 %copy.12 = bf16[1,1024,512]{2,1,0:T(8,128)(2,1)} copy(bf16[1,1024,512]{2,1,0:T(8,128)(2,1)} %bitcast.4) | data formatting | bytes 2097152

commit v4 on v3

--- a/solution.py
+++ b/solution.py
@@ -233,6 +233,15 @@
         each(1, users, one)
 
     forward(0)
+    def pass_on(ch):
+        relay(ch, 0).start()
+        forward(ch)
+
+    @pl.when(c == 0)
+    def _():
+        pass_on(1)
+        pass_on(2)
+
     id_keep.wait()
     id_send.wait()
     each(0, users, lambda k: incoming(0, k).wait_recv())
@@ -250,16 +259,12 @@
 
     @pl.when(c == 0)
     def _():
-        def pass_on(ch):
-            relay(ch, 0).start()
-            forward(ch)
-
         each(0, part, project_block)
-        pass_on(1)
+        pass_on(3)
         each(part, strips, project_block)
         for s in range(strips):
-            if s + 2 <= strips:
-                pass_on(s + 2)
+            if s + 4 <= strips:
+                pass_on(s + 4)
             strip(s, True)
         each(1, strips + 1, lambda ch: each(0, users, lambda k: relay(ch, k).wait_send()))
 

time: 65.9 us -> 62.2 us (0.944)
  Pallas kernels: 60 us -> 56.2 us
    pallas_call x1, Pallas kernels: 60 us -> 56.2 us  [fused(): pl.pallas_call(functools.partial(fused_kernel, users), out_shape=jax.Shap...]
where the time goes in v4:
time: 62.2 us; the launch traced here: 61.9 us
  Pallas kernels  56.2 us (90%)
  local copies, waits for them, and re-layouts  5.04 us (8%)
  between operations  0.66 us (1%)
    pallas_call x1, Pallas kernels, fused(): pl.pallas_call(functools.partial(fused_kernel, users), out_shape=jax.Shap...  56.2 us
    unnamed x2, local copies, waits for them, and re-layouts  5.04 us

profile of v4, /device:TPU:15, one launch (start us, length us, event | category | flops | bytes accessed | tf_op | source)
XLA Modules:
  0.0 61.9 jit_solution(8345532385898279095)
XLA Ops:
  0.7 2.8 %copy.9 = bf16[16,16,2048]{2,0,1:T(8,128)(2,1)} copy(bf16[16,16,2048]{2,1,0:T(8,128)(2,1)} %param.6) | data formatting | bytes 2097152 | tf_op args[0]
  3.4 56.2 %fused.1 = bf16[1024,512]{1,0:T(8,128)(2,1)} custom-call(bf16[16,16,2048]{2,1,0:T(8,128)(2,1)} %bitcast.5, s32[1,1024]{1,0:T(1,128)} %bucket.1, f32[128,512]{1,0:T(8,128)} %table.1, s32[1]{0:T(128)S(6)} %copy.11.length, bf16[512,2048]{1,0:T(8,128)(2,1)} %w_proj.1, bf16[512,512]{1,0:T(8,128)(2,1)} %w_out.1), custom_call_target="tpu_custom_call" | custom-call | tf_op jit(solution)/shard_map/fused/pallas_call | solution.py:295
  59.7 2.3 %copy.12 = bf16[1,1024,512]{2,1,0:T(8,128)(2,1)} copy(bf16[1,1024,512]{2,1,0:T(8,128)(2,1)} %bitcast.4) | data formatting | bytes 2097152
